TPU v7x, 32 devices: a whole 2x2x4 slice. The times are simulated.
32 devices in a mesh: tm: 2 (over x), cells: 16 (over z, y, core).
Axes of the slice: x: 2, y: 2, z: 4, core: 2. Of those that a mesh axis runs over, the one named last changes fastest.
Arguments:
- filtered: float32 [2, 8192], P('tm', 'cells'), may hold values from -6 to 6
- panels: bfloat16 [2, 8192, 512], P('tm', 'cells'), may hold values from -0.59662135 to 0.59662135
- tiles: bfloat16 [32, 9, 256, 256], P('cells'), may hold values from -0.06666667 to 1.0666667
- neighbours: int32 [32, 9], P('cells'), may hold values from 0 to 31, as said below
- noise_var: float32 [8192], P('cells'), may hold values from 0.5 to 8
- end_smoothed: float32 [8192], P('cells'), may hold values from -6 to 6
Outputs:
- smoothed: float32 [2, 8192], P('tm', 'cells')
Inputs may be any that keep to these rules, and one draw needn't show every extreme that they name: `neighbours`: each block row b names 9 distinct block columns, b among them, all within the 10 consecutive blocks, counted cyclically over 32, that begin at block (b // 2 - 2) * 2.
All inputs are finite; a program needn't handle non-finite values.
Results may differ from a plain program's by a relative error of at most 0.00045.
Values may be sent and summed in bfloat16 or wider, within the bound.
A program may use at most 64 MiB of HBM per device.

v0:
```python
import jax
import jax.numpy as jnp
from jax import lax
from jax.sharding import PartitionSpec as P

maximal_precision = lax.Precision.HIGHEST


def passed_along(value, axis, by):
    size = lax.axis_size(axis)
    return lax.ppermute(value, axis, [(i, (i + by) % size) for i in range(size)])


def passed_along_2(value, axis, steps):
    count = lax.axis_size(axis)
    leading, last = (max(0, -steps), min(count, count - steps))
    return lax.ppermute(value, axis, [(source, source + steps) for source in range(leading, last)])


def cholesky_apply(factor, right_side):
    column = right_side[:, None]
    halfway = lax.linalg.triangular_solve(factor, column, left_side=True, lower=True)
    solved = lax.linalg.triangular_solve(
        factor, halfway, left_side=True, lower=True, transpose_a=True
    )
    return solved[:, 0]


def project_onto_rank(scaled_rows, vector):
    return lax.psum(jnp.dot(vector, scaled_rows, precision=maximal_precision), "cells")


def per_device(filtered, panels, tiles, neighbours, noise_var, end_smoothed):
    steps_here, cells_here, rank_width = panels.shape
    blocks_here = tiles.shape[0]
    block_cells = tiles.shape[2]
    cell_devices = lax.axis_size("cells")
    time_devices = lax.axis_size("tm")
    block_total = blocks_here * cell_devices
    window_first = (lax.axis_index("cells") - 2) * blocks_here
    position = jnp.mod(neighbours - window_first, block_total)
    rounded_means = filtered.astype(jnp.bfloat16)
    pieces = {0: (panels, rounded_means)}
    for heading in (-1, 1):
        adjacent = passed_along((panels, rounded_means), "cells", -heading)
        pieces[heading] = adjacent
        pieces[2 * heading] = passed_along((adjacent[0], adjacent[1]), "cells", -heading)
    window_panels = jnp.concatenate(
        [
            pieces[offset][0].reshape(steps_here, blocks_here, block_cells, rank_width)
            for offset in (-2, -1, 0, 1, 2)
        ],
        axis=1,
    )
    window_means = jnp.concatenate(
        [
            pieces[offset][1].reshape(steps_here, blocks_here, block_cells)
            for offset in (-2, -1, 0, 1, 2)
        ],
        axis=1,
    )
    advected = jnp.einsum(
        "rkij,trkjc->tric", tiles, window_panels[:, position], preferred_element_type=jnp.float32
    ).reshape(steps_here, cells_here, rank_width)
    predicted_state = jnp.einsum(
        "rkij,trkj->tri", tiles, window_means[:, position], preferred_element_type=jnp.float32
    ).reshape(steps_here, cells_here)
    rescaled_rows = advected / noise_var[None, :, None]
    local_gram = jnp.einsum("tnc,tnd->tcd", advected, rescaled_rows, precision=maximal_precision)
    summed = lax.psum(local_gram, "cells")
    system = summed + jnp.eye(rank_width, dtype=jnp.float32)[None]
    factor_list = [jnp.linalg.cholesky(system[0])]

    def sweep(boundary):
        subsequent_value = boundary
        results = [None] * steps_here
        for step_lookup in reversed(range(steps_here)):
            coefficient = cholesky_apply(
                factor_list[step_lookup],
                project_onto_rank(
                    rescaled_rows[step_lookup], subsequent_value - predicted_state[step_lookup]
                ),
            )
            subsequent_value = filtered[step_lookup] + jnp.dot(
                panels[step_lookup].astype(jnp.float32), coefficient, precision=maximal_precision
            )
            results[step_lookup] = subsequent_value
        return jnp.stack(results)

    last_section = lax.axis_index("tm") == time_devices - 1

    def relay_turn(turn, boundary):
        received = passed_along_2(sweep(boundary)[0], "tm", -1)
        return jnp.where(last_section, end_smoothed, received)

    start_state = jnp.where(last_section, end_smoothed, jnp.zeros_like(end_smoothed))
    boundary = lax.fori_loop(0, time_devices - 1, relay_turn, start_state)
    return sweep(boundary)


def solution(mesh):
    placed = (
        P("tm", "cells"),
        P("tm", "cells", None),
        P("cells", None, None, None),
        P("cells", None),
        P("cells"),
        P("cells"),
    )
    return jax.shard_map(
        per_device, mesh=mesh, in_specs=placed, out_specs=P("tm", "cells"), check_vma=False
    )
```

profile of v0, /device:TPU:0, one launch (start us, length us, event | category | flops | bytes accessed | tf_op | source)
XLA Modules:
  0.0 395.1 jit_solution(2597715061365446344)
XLA Ops:
  7.1 5.0 %collective-permute-start.2 = (bf16[1,512,512]{2,1,0:T(8,128)(2,1)}, bf16[1,512,512]{2,1,0:T(8,128)(2,1)S(1)}, u32[]{:S(2)}, u32[]{:S(2)}) collective-permute-start(bf16[1,512,512]{2,1,0:T(8,128)(2,1)} %param.11), channel_id=1, source_target_pairs={{0,15},{1,0},{2,1},{3,2},{4,3},{5,4},{6,5},{7,6},{8,7},{9,8},{10,9... | collective-permute-start | bytes 1572872 | tf_op jit(solution)/shard_map/ppermute | solution.py:11
  12.8 4.4 %collective-permute-start.6 = (bf16[1,512]{1,0:T(2,128)(2,1)S(1)}, bf16[1,512]{1,0:T(2,128)(2,1)S(1)}, u32[]{:S(2)}, u32[]{:S(2)}) collective-permute-start(bf16[1,512]{1,0:T(2,128)(2,1)S(1)} %convert_element_type.17), channel_id=1, source_target_pairs={{0,15},{1,0},{2,1},{3,2},{4,3},{5,4},{6,5},{7,6},{8,7},{9,8},{10,9... | collective-permute-start | bytes 3080 | tf_op jit(solution)/shard_map/ppermute | solution.py:11
  19.4 2.4 collective-permute-start.1
  22.4 2.5 collective-permute-start.5
  24.9 2.0 collective-permute-start.7
  27.6 3.4 collective-permute-done.5
  32.5 1.7 collective-permute-start.3
  34.2 1.9 constant_dynamic-update-slice_fusion.4
  36.1 1.9 constant_dynamic-update-slice_fusion.3
  39.7 1.2 collective-permute-done.3
  41.8 5.6 %gather_fusion = bf16[18,256,512]{2,1,0:T(8,128)(2,1)} fusion(bf16[10,256,512]{2,1,0:T(8,128)(2,1)} %bitcast.6, s32[1024]{0:T(1024)S(1)} %pad_clamp_fusion), kind=kCustom, calls=%fused_computation | custom fusion | bytes 9437256 | tf_op jit(solution)/shard_map/gather | solution.py:63
  47.4 3.7 fusion.105
  52.1 3.0 convolution_bitcast_fusion
  55.1 1.4 bitcast_divide_fusion
  57.1 34.6 %psum.23 = f32[512,1]{0,1:T(1,128)S(1)} all-reduce(f32[512,1]{0,1:T(1,128)S(1)} %convolution_bitcast_fusion.2), channel_id=1, replica_groups=mesh['tm'=2,'cells'=16] {'cells'}, use_global_device_ids=true, to_apply=%region_9.10 | all-reduce | flops 512 | bytes 4096 | tf_op jit(solution)/shard_map/while/body/eval_jaxpr/psum | solution.py:30
  91.7 58.8 %all-reduce.3.cloned.1.call-done = f32[1,512,512]{1,2,0:T(8,128)} async-done(((f32[1,512,512]{1,2,0:T(8,128)}), f32[1,512,512]{1,2,0:T(8,128)}) %all-reduce.3.cloned.1.call-update) | async-done | bytes 1048592 | tf_op jit(solution)/shard_map/psum | solution.py:70
  150.5 2.3 fusion.15
  152.8 2.6 copy.12
  155.4 1.8 fusion.12
  158.2 11.7 %cholesky.104 = f32[128,128]{1,0:T(8,128)S(1)} custom-call(f32[128,128]{1,0:T(8,128)S(1)} %cholesky.266), custom_call_target="Cholesky" | custom-call | tf_op jit(solution)/shard_map/jit(cholesky)/cholesky | solution.py:72
  169.9 1.2 select_reduce_fusion.3
  171.1 10.6 %custom-call.33 = f32[1,128,128]{1,2,0:T(8,128)S(1)} custom-call(f32[1,128,128]{2,1,0:T(8,128)} %get-tuple-element.85), custom_call_target="InvertDiagBlocksLowerTriangular" | custom-call | tf_op jit(solution)/shard_map/jit(cholesky)/cholesky | solution.py:72
  182.9 2.0 constant_dynamic-update-slice_fusion.8
  184.9 1.2 convolution_subtract_fusion
  186.8 11.7 %cholesky.217 = f32[128,128]{1,0:T(8,128)S(1)} custom-call(f32[128,128]{1,0:T(8,128)S(1)} %cholesky.270), custom_call_target="Cholesky" | custom-call | tf_op jit(solution)/shard_map/jit(cholesky)/cholesky | solution.py:72
  199.7 10.0 %custom-call.34 = f32[1,128,128]{1,2,0:T(8,128)S(1)} custom-call(f32[1,128,128]{2,1,0:T(8,128)S(1)} %get-tuple-element.82), custom_call_target="InvertDiagBlocksLowerTriangular" | custom-call | tf_op jit(solution)/shard_map/jit(cholesky)/cholesky | solution.py:72
  209.7 1.8 convolution_dynamic-update-slice_fusion
  211.5 1.4 convolution_subtract_fusion.1
  213.6 13.2 %cholesky.238 = f32[128,128]{1,0:T(8,128)} custom-call(f32[128,128]{1,0:T(8,128)} %cholesky.275), custom_call_target="Cholesky" | custom-call | tf_op jit(solution)/shard_map/jit(cholesky)/cholesky | solution.py:72
  226.7 1.5 select_reduce_fusion.1
  229.0 11.3 %custom-call.35 = f32[1,128,128]{1,2,0:T(8,128)} custom-call(f32[1,128,128]{2,1,0:T(8,128)} %get-tuple-element.79), custom_call_target="InvertDiagBlocksLowerTriangular" | custom-call | tf_op jit(solution)/shard_map/jit(cholesky)/cholesky | solution.py:72
  240.2 1.7 convolution_dynamic-update-slice_fusion.1
  241.9 1.4 convolution_subtract_fusion.2
  243.3 11.7 %cholesky.255 = f32[128,128]{1,0:T(8,128)S(1)} custom-call(f32[128,128]{1,0:T(8,128)S(1)} %convolution_subtract_fusion.2), custom_call_target="Cholesky" | custom-call | tf_op jit(solution)/shard_map/jit(cholesky)/cholesky | solution.py:72
  256.6 1.4 compare_reduce_fusion.2
  260.6 2.4 select_select_fusion
  263.7 14.1 %while.12 = (s32[]{:T(128)}, f32[512,512]{1,0:T(8,128)}, s32[4,2]{0,1:T(2,128)S(1)}, f32[4,128,128]{2,1,0:T(8,128)}, s32[]{:T(128)}) while((s32[]{:T(128)}, f32[512,512]{1,0:T(8,128)}, s32[4,2]{0,1:T(2,128)S(1)}, f32[4,128,128]{2,1,0:T(8,128)}, s32[]{:T(128)}) %tuple.42), condition=%wide.while_cond.1.clone, body=%wide.while_body.1.clone.sunk | while | flops 2 | bytes 132705 | solution.py:23
  264.3 2.9 bitcast_dynamic-update-slice_fusion.2
  267.9 2.9 bitcast_dynamic-update-slice_fusion.2
  271.4 2.9 bitcast_dynamic-update-slice_fusion.2
  274.9 2.8 bitcast_dynamic-update-slice_fusion.2
  277.8 40.7 %custom-call.41 = f32[4,128,128]{1,2,0:T(8,128)} custom-call(f32[4,128,128]{2,1,0:T(8,128)} %get-tuple-element.65), custom_call_target="InvertDiagBlocksLowerTriangular" | custom-call | tf_op jit(solution)/shard_map/triangular_solve/custom-call.0 | solution.py:23
  331.2 1.2 fusion.10
  333.4 1.6 fusion.18
  335.1 1.3 collective-permute-start.8
  336.4 4.2 %collective-permute-done.8 = f32[512]{0:T(512)S(1)} collective-permute-done((f32[512]{0:T(512)S(1)}, f32[512]{0:T(512)S(1)}, u32[]{:S(2)}, u32[]{:S(2)}) %collective-permute-start.8) | collective-permute-done | bytes 2080 | tf_op jit(solution)/shard_map/while/body/eval_jaxpr/ppermute | solution.py:17
  341.1 29.5 %psum.24 = f32[512,1]{0,1:T(1,128)S(1)} all-reduce(f32[512,1]{0,1:T(1,128)S(1)} %convolution_bitcast_fusion.1), channel_id=1, replica_groups=mesh['tm'=2,'cells'=16] {'cells'}, use_global_device_ids=true, to_apply=%region_10.13 | all-reduce | flops 512 | bytes 4096 | tf_op jit(solution)/shard_map/psum | solution.py:30
  385.6 1.6 fusion.16
  (102 shorter events, 50.4 us)
Async XLA Ops:
  6.5 25.2 %copy-start = (bf16[2,9,256,256]{3,2,1,0:T(8,128)(2,1)S(1)}, bf16[2,9,256,256]{3,2,1,0:T(8,128)(2,1)}, u32[]{:S(2)}) copy-start(bf16[2,9,256,256]{3,2,1,0:T(8,128)(2,1)} %param.12) | copy-start | bytes 7077892
  6.5 31.5 %copy-start.1 = (bf16[1,512,512]{2,1,0:T(8,128)(2,1)S(1)}, bf16[1,512,512]{2,1,0:T(8,128)(2,1)}, u32[]{:S(2)}) copy-start(bf16[1,512,512]{2,1,0:T(8,128)(2,1)} %param.11) | copy-start | bytes 1572868
  6.5 27.7 %copy-start.7 = (f32[512]{0:T(512)S(1)}, f32[512]{0:T(512)}, u32[]{:S(2)}) copy-start(f32[512]{0:T(512)} %param.15) | copy-start | bytes 6148
  6.5 144.0 %all-reduce.3.cloned.1.call-start = ((), (), s32[]{:S(2)}) async-start(), calls=%async_computation | async-start | bytes 2097152 | tf_op jit(solution)/shard_map/psum | solution.py:70
  6.5 12.8 %collective-permute-start = (bf16[1,512,512]{2,1,0:T(8,128)(2,1)}, bf16[1,512,512]{2,1,0:T(8,128)(2,1)}, u32[]{:S(2)}, u32[]{:S(2)}) collective-permute-start(bf16[1,512,512]{2,1,0:T(8,128)(2,1)} %param.11), channel_id=1, source_target_pairs={{0,1},{1,2},{2,3},{3,4},{4,5},{5,6},{6,7},{7,8},{8,9},{9,10},{10,1... | collective-permute-start | bytes 1572872 | tf_op jit(solution)/shard_map/ppermute | solution.py:11
  7.1 25.4 %collective-permute-start.2 = (bf16[1,512,512]{2,1,0:T(8,128)(2,1)}, bf16[1,512,512]{2,1,0:T(8,128)(2,1)S(1)}, u32[]{:S(2)}, u32[]{:S(2)}) collective-permute-start(bf16[1,512,512]{2,1,0:T(8,128)(2,1)} %param.11), channel_id=1, source_target_pairs={{0,15},{1,0},{2,1},{3,2},{4,3},{5,4},{6,5},{7,6},{8,7},{9,8},{10,9... | collective-permute-start | bytes 1572872 | tf_op jit(solution)/shard_map/ppermute | solution.py:11
  12.8 9.5 %collective-permute-start.4 = (bf16[1,512]{1,0:T(2,128)(2,1)S(1)}, bf16[1,512]{1,0:T(2,128)(2,1)S(1)}, u32[]{:S(2)}, u32[]{:S(2)}) collective-permute-start(bf16[1,512]{1,0:T(2,128)(2,1)S(1)} %convert_element_type.17), channel_id=1, source_target_pairs={{0,1},{1,2},{2,3},{3,4},{4,5},{5,6},{6,7},{7,8},{8,9},{9,10},{10,1... | collective-permute-start | bytes 3080 | tf_op jit(solution)/shard_map/ppermute | solution.py:11
  12.8 12.0 %collective-permute-start.6 = (bf16[1,512]{1,0:T(2,128)(2,1)S(1)}, bf16[1,512]{1,0:T(2,128)(2,1)S(1)}, u32[]{:S(2)}, u32[]{:S(2)}) collective-permute-start(bf16[1,512]{1,0:T(2,128)(2,1)S(1)} %convert_element_type.17), channel_id=1, source_target_pairs={{0,15},{1,0},{2,1},{3,2},{4,3},{5,4},{6,5},{7,6},{8,7},{9,8},{10,9... | collective-permute-start | bytes 3080 | tf_op jit(solution)/shard_map/ppermute | solution.py:11
  19.4 14.9 %collective-permute-start.1 = (bf16[1,512,512]{2,1,0:T(8,128)(2,1)}, bf16[1,512,512]{2,1,0:T(8,128)(2,1)}, u32[]{:S(2)}, u32[]{:S(2)}) collective-permute-start(bf16[1,512,512]{2,1,0:T(8,128)(2,1)} %collective-permute-done), channel_id=1, source_target_pairs={{0,1},{1,2},{2,3},{3,4},{4,5},{5,6},{6,7},{7,8},{8,9},{9,10},{10,1... | collective-permute-start | bytes 1572872 | tf_op jit(solution)/shard_map/ppermute | solution.py:11
  22.4 8.6 %collective-permute-start.5 = (bf16[1,512]{1,0:T(2,128)(2,1)S(1)}, bf16[1,512]{1,0:T(2,128)(2,1)S(1)}, u32[]{:S(2)}, u32[]{:S(2)}) collective-permute-start(bf16[1,512]{1,0:T(2,128)(2,1)S(1)} %collective-permute-done.4), channel_id=1, source_target_pairs={{0,1},{1,2},{2,3},{3,4},{4,5},{5,6},{6,7},{7,8},{8,9},{9,10},{10,1... | collective-permute-start | bytes 3080 | tf_op jit(solution)/shard_map/ppermute | solution.py:11
  24.9 6.2 %collective-permute-start.7 = (bf16[1,512]{1,0:T(2,128)(2,1)S(1)}, bf16[1,512]{1,0:T(2,128)(2,1)S(1)}, u32[]{:S(2)}, u32[]{:S(2)}) collective-permute-start(bf16[1,512]{1,0:T(2,128)(2,1)S(1)} %collective-permute-done.6), channel_id=1, source_target_pairs={{0,15},{1,0},{2,1},{3,2},{4,3},{5,4},{6,5},{7,6},{8,7},{9,8},{10,9... | collective-permute-start | bytes 3080 | tf_op jit(solution)/shard_map/ppermute | solution.py:11
  32.5 8.4 %collective-permute-start.3 = (bf16[1,512,512]{2,1,0:T(8,128)(2,1)S(1)}, bf16[1,512,512]{2,1,0:T(8,128)(2,1)S(1)}, u32[]{:S(2)}, u32[]{:S(2)}) collective-permute-start(bf16[1,512,512]{2,1,0:T(8,128)(2,1)S(1)} %collective-permute-done.2), channel_id=1, source_target_pairs={{0,15},{1,0},{2,1},{3,2},{4,3},{5,4},{6,5},{7,6},{8,7},{9,8},{10,9... | collective-permute-start | bytes 1572872 | tf_op jit(solution)/shard_map/ppermute | solution.py:11
  51.1 1.0 copy-start.3
  52.1 3.0 copy-start.6
  157.2 1.0 copy-start.2
  186.1 0.7 copy-start.4
  241.9 93.1 %copy-start.5 = (f32[1,512]{1,0:T(1,128)S(1)}, f32[1,512]{1,0:T(1,128)}, u32[]{:S(2)}) copy-start(f32[1,512]{1,0:T(1,128)} %param.10) | copy-start | bytes 6148
  335.1 5.5 %collective-permute-start.8 = (f32[512]{0:T(512)S(1)}, f32[512]{0:T(512)S(1)}, u32[]{:S(2)}, u32[]{:S(2)}) collective-permute-start(f32[512]{0:T(512)S(1)} %add.73), channel_id=1, source_target_pairs={{16,0},{17,1},{18,2},{19,3},{20,4},{21,5},{22,6},{23,7},{24,8},{25... | collective-permute-start | bytes 6152 | tf_op jit(solution)/shard_map/while/body/eval_jaxpr/ppermute | solution.py:17
Sparse Core Ops, SparseCore 0:
  55.2 95.2 all-reduce.2
where the time goes:
time: 402 us; the launch traced here: 395 us
  other arithmetic  140 us (35%)
  waiting for transfers between devices  68.2 us (17%)
  blocking collectives  64.1 us (16%)
  matrix products  51.3 us (13%)
  local copies, waits for them, and re-layouts  35.3 us (9%)
  starting transfers between devices  19.9 us (5%)
  between operations  16.7 us (4%)
    another operation x14, other arithmetic, per_device(): factor_list = [jnp.linalg.cholesky(system[0])]  87.7 us
    psum x2, blocking collectives, project_onto_rank(): lax.psum(jnp.dot(vector, scaled_rows, precision=maximal_precision), 'cells')  64.1 us
    psum x1, waiting for transfers between devices, per_device(): summed = lax.psum(local_gram, 'cells')  58.8 us
    another operation x4, other arithmetic, cholesky_apply(): lax.linalg.triangular_solve(factor, halfway, left_side=True, lower=True,...  43.7 us
    ppermute x8, starting transfers between devices, passed_along(): lax.ppermute(value, axis, [(i, (i + by) % size) for i in range(size)])  18.6 us
    another operation x14, matrix products, cholesky_apply(): lax.linalg.triangular_solve(factor, halfway, left_side=True, lower=True,...  15 us
    another operation x14, matrix products, cholesky_apply(): lax.linalg.triangular_solve(factor, column, left_side=True, lower=True)  14.9 us
    another operation x13, local copies, waits for them, and re-layouts, cholesky_apply(): lax.linalg.triangular_solve(factor, halfway, left_side=True, lower=True,...  14.8 us
  transfers between devices with their start and end apart: 10, of which 5 were waited for; matrix products, arithmetic and copies ran while one was open for 3% of the time, Pallas kernels for 0%

commit v1 on v0

v1 whole, which is shorter than its diff:
```python
import functools
import jax
import jax.numpy as jnp
from jax import lax
from jax.experimental import pallas as pl
from jax.experimental.pallas import tpu as pltpu
from jax.sharding import PartitionSpec as P

HI = lax.Precision.HIGHEST
B = 128
MESH = pl.DeviceIdType.MESH


def invert_block(s, n):
    groups = n // 8
    rows = [s[8 * g:8 * g + 8, :] for g in range(groups)]
    lane = lax.broadcasted_iota(jnp.int32, (8, n), 1)
    sub = lax.broadcasted_iota(jnp.int32, (8, n), 0)
    spread = lambda v, j: jnp.broadcast_to(v[j:j + 1, :], (8, n))
    for g in range(groups):
        k = 8 * g
        cols = [[jnp.broadcast_to(rows[i][:, k + j:k + j + 1], (8, n)) for i in range(groups)] for j in range(8)]
        inside = (lane >= k) & (lane < k + 8)
        lead = jnp.where(inside, jnp.where(lane - k == sub, 1.0, 0.0), rows[g])
        d = [cols[j][g] for j in range(8)]
        for j in range(8):
            inverse = 1.0 / spread(d[j], j)
            fresh = spread(lead, j) * inverse
            lead = jnp.where(sub == j, fresh, lead - d[j] * fresh)
            for l in range(j + 1, 8):
                moved = spread(d[l], j) * inverse
                d[l] = jnp.where(sub == j, moved, d[l] - d[j] * moved)
        spreads = [spread(lead, j) for j in range(8)]
        for i in range(groups):
            if i == g:
                continue
            a = jnp.where(inside, 0.0, rows[i])
            b = cols[4][i] * spreads[4]
            for j in range(4):
                a = a - cols[j][i] * spreads[j]
            for j in range(5, 8):
                b = b + cols[j][i] * spreads[j]
            rows[i] = a - b
        rows[g] = lead
    return jnp.concatenate(rows, axis=0)

def inverse_kernel(s_ref, o_ref, w_ref):
    rank = s_ref.shape[-1]
    n = 128
    o_ref[...] = s_ref[...]
    def step(b, _):
        at = pl.multiple_of(b * n, n)
        own = pl.ds(at, n)
        small = invert_block(o_ref[own, own], n)
        w = jnp.dot(small, o_ref[own, :], precision=HI, preferred_element_type=jnp.float32)
        w_ref[...] = w
        w_ref[:, own] = small
        column = o_ref[:, own]
        o_ref[:, own] = jnp.zeros((rank, n), jnp.float32)
        full = jnp.dot(column, w_ref[...], precision=HI, preferred_element_type=jnp.float32)
        o_ref[...] = o_ref[...] - full
        o_ref[own, :] = w_ref[...]
        return 0
    lax.fori_loop(0, rank // n, step, 0)

def inverse(s):
    r = s.shape[-1]
    return pl.pallas_call(inverse_kernel, out_shape=jax.ShapeDtypeStruct((r, r), jnp.float32),
        in_specs=[pl.BlockSpec(memory_space=pltpu.VMEM)], out_specs=pl.BlockSpec(memory_space=pltpu.VMEM),
        scratch_shapes=[pltpu.VMEM((128, r), jnp.float32)],
        compiler_params=pltpu.CompilerParams(vmem_limit_bytes=40 << 20))(s)

def block_pairs(rank):
    count = rank // B
    return [[p for p in range(count // 2) if p % 2 == half] for half in (0, 1)]


def gram_kernel(n, adv_ref, noise_ref, out_ref, scaled, packed, landed, parts, slots, reduced, gathered, other, sems, sems_chip):
    me = lax.axis_index("cells")
    steps, cells, rank = adv_ref.shape
    count = rank // B
    pairs = block_pairs(rank)
    chips = n // 2
    chip, core = me // 2, me % 2
    partner = chip * 2 + (1 - core)
    rows = packed.shape[2] // steps

    barrier = pltpu.get_barrier_semaphore()
    for k in range(1, n):
        pl.semaphore_signal(barrier, inc=1, device_id={"cells": (me + k) % n}, device_id_type=MESH)

    for t in range(steps):
        scaled[...] = adv_ref[t] / noise_ref[...]
        for half in (0, 1):
            for at, p in enumerate(pairs[half]):
                long, short = count - 1 - p, p
                pieces = []
                for r in (long, short):
                    pieces.append(
                        lax.dot_general(
                            scaled[:, r * B : (r + 1) * B],
                            adv_ref[t, :, : (r + 1) * B],
                            (((0,), (0,)), ((), ())),
                            precision=HI,
                            preferred_element_type=jnp.float32,
                        )
                    )
                value = jnp.concatenate(pieces, axis=1)
                per = B * len(pairs[half]) // chips
                for q in range(B // per):
                    packed[half, at * (B // per) + q, t * rows : t * rows + per] = value[q * per : (q + 1) * per]
    pl.semaphore_wait(barrier, n - 1)

    first = pltpu.make_async_remote_copy(
        packed.at[1 - core], landed, sems.at[0], sems.at[1], device_id={"cells": partner}, device_id_type=MESH
    )
    first.start()
    first.wait()
    parts[...] = packed[core] + landed[...]

    def spread(k):
        q = (chip + k) % chips
        return pltpu.make_async_remote_copy(
            parts.at[q], slots.at[k], sems_chip.at[0, k], sems_chip.at[1, k],
            device_id={"cells": q * 2 + core}, device_id_type=MESH,
        )

    def collect(k):
        q = (chip + k) % chips
        return pltpu.make_async_remote_copy(
            reduced, gathered.at[chip], sems_chip.at[2, k], sems_chip.at[3, k],
            device_id={"cells": q * 2 + core}, device_id_type=MESH,
        )

    for k in range(1, chips):
        spread(k).start()
    total = parts[chip]
    for k in range(1, chips):
        spread(k).wait()
        total = total + slots[k]
    reduced[...] = total
    for k in range(1, chips):
        collect(k).start()
    gathered[chip] = total
    for k in range(1, chips):
        collect(k).wait()
    second = pltpu.make_async_remote_copy(
        gathered, other, sems.at[2], sems.at[3], device_id={"cells": partner}, device_id_type=MESH
    )
    second.start()
    second.wait()

    eye = jnp.where(
        lax.broadcasted_iota(jnp.int32, (B, B), 0) == lax.broadcasted_iota(jnp.int32, (B, B), 1), 1.0, 0.0
    )

    def unpack(half, ref):
        each = chips // len(pairs[half])
        for t in range(steps):
            for at, p in enumerate(pairs[half]):
                value = jnp.concatenate(
                    [ref[at * each + q, t * rows : (t + 1) * rows] for q in range(each)], axis=0
                )
                long, short = count - 1 - p, p
                for r, begin in ((long, 0), (short, (long + 1) * B)):
                    for c in range(r + 1):
                        block = value[:, begin + c * B : begin + (c + 1) * B]
                        if c == r:
                            block = block + eye
                        else:
                            out_ref[t, c * B : (c + 1) * B, r * B : (r + 1) * B] = block.T
                        out_ref[t, r * B : (r + 1) * B, c * B : (c + 1) * B] = block

    @pl.when(core == 0)
    def _():
        unpack(0, gathered)
        unpack(1, other)

    @pl.when(core == 1)
    def _():
        unpack(1, gathered)
        unpack(0, other)


def summed_system(advected, noise_var, n):
    steps, cells, rank = advected.shape
    chips = n // 2
    per_half = (rank // B) // 4
    rows = B * per_half // chips * steps
    wide = rank + B
    f32 = jnp.float32
    return pl.pallas_call(
        functools.partial(gram_kernel, n),
        out_shape=jax.ShapeDtypeStruct((steps, rank, rank), f32),
        in_specs=[pl.BlockSpec(memory_space=pltpu.VMEM)] * 2,
        out_specs=pl.BlockSpec(memory_space=pltpu.VMEM),
        scratch_shapes=[
            pltpu.VMEM((cells, rank), f32),
            pltpu.VMEM((2, chips, rows, wide), f32),
            pltpu.VMEM((chips, rows, wide), f32),
            pltpu.VMEM((chips, rows, wide), f32),
            pltpu.VMEM((chips, rows, wide), f32),
            pltpu.VMEM((rows, wide), f32),
            pltpu.VMEM((chips, rows, wide), f32),
            pltpu.VMEM((chips, rows, wide), f32),
            pltpu.SemaphoreType.DMA((4,)),
            pltpu.SemaphoreType.DMA((4, chips)),
        ],
        compiler_params=pltpu.CompilerParams(collective_id=0, has_side_effects=True, vmem_limit_bytes=56 << 20),
    )(advected, noise_var[:, None])


def split3(v):
    a = v.astype(jnp.bfloat16)
    rest = v - a.astype(jnp.float32)
    b = rest.astype(jnp.bfloat16)
    c = (rest - b.astype(jnp.float32)).astype(jnp.bfloat16)
    return a, b, c


def sweep_kernel(n, sections, adv_ref, inv_ref, pan_ref, pred_ref, filt_ref, noise_ref, end_ref, out_ref,
                 later, mine, seen, passed, sem_send, sem_recv, sem_tm):
    me = lax.axis_index("cells")
    section = lax.axis_index("tm")
    steps = adv_ref.shape[0]
    has_next = section < sections - 1
    has_before = section > 0

    barrier = pltpu.get_barrier_semaphore()
    for k in range(1, n):
        pl.semaphore_signal(barrier, inc=1, device_id={"cells": (me + k) % n}, device_id_type=MESH)

    @pl.when(has_next)
    def _():
        pl.semaphore_signal(barrier, inc=1, device_id={"tm": section + 1}, device_id_type=MESH)

    @pl.when(has_before)
    def _():
        pl.semaphore_signal(barrier, inc=1, device_id={"tm": section - 1}, device_id_type=MESH)

    pl.semaphore_wait(barrier, n - 1 + has_next.astype(jnp.int32) + has_before.astype(jnp.int32))

    def handoff():
        return pltpu.make_async_remote_copy(
            later, passed, sem_tm.at[0], sem_tm.at[1], device_id={"tm": section - 1}, device_id_type=MESH
        )

    @pl.when(has_next)
    def _():
        handoff().wait_recv()
        later[...] = passed[...]

    @pl.when(section == sections - 1)
    def _():
        later[...] = end_ref[...]

    for t in reversed(range(steps)):
        gap = (later[...] - pred_ref[t : t + 1]) / noise_ref[...]
        mine[t] = jnp.dot(gap, adv_ref[t], precision=HI, preferred_element_type=jnp.float32)

        def share(k):
            return pltpu.make_async_remote_copy(
                mine.at[t], seen.at[t, me], sem_send.at[t, k], sem_recv.at[t, k],
                device_id={"cells": (me + k) % n}, device_id_type=MESH,
            )

        for k in range(1, n):
            share(k).start()
        seen[t, me] = mine[t]
        for k in range(1, n):
            share(k).wait()
        total = seen[t, 0]
        for k in range(1, n):
            total = total + seen[t, k]
        coefficient = jnp.dot(total, inv_ref[t], precision=HI, preferred_element_type=jnp.float32)
        moved = sum(
            lax.dot_general(c, pan_ref[t], (((1,), (1,)), ((), ())), preferred_element_type=jnp.float32)
            for c in split3(coefficient)
        )
        result = filt_ref[t : t + 1] + moved
        later[...] = result
        out_ref[t : t + 1] = result

    @pl.when(has_before)
    def _():
        handoff().start()
        handoff().wait_send()


def sweep_back(advected, inverses, panels, predicted, filtered, noise_var, end_smoothed, n, sections):
    steps, cells, rank = advected.shape
    f32 = jnp.float32
    return pl.pallas_call(
        functools.partial(sweep_kernel, n, sections),
        out_shape=jax.ShapeDtypeStruct((steps, cells), f32),
        in_specs=[pl.BlockSpec(memory_space=pltpu.VMEM)] * 7,
        out_specs=pl.BlockSpec(memory_space=pltpu.VMEM),
        scratch_shapes=[
            pltpu.VMEM((1, cells), f32),
            pltpu.VMEM((steps, 1, rank), f32),
            pltpu.VMEM((steps, n, 1, rank), f32),
            pltpu.VMEM((1, cells), f32),
            pltpu.SemaphoreType.DMA((steps, n)),
            pltpu.SemaphoreType.DMA((steps, n)),
            pltpu.SemaphoreType.DMA((2,)),
        ],
        compiler_params=pltpu.CompilerParams(collective_id=1, has_side_effects=True, vmem_limit_bytes=40 << 20),
    )(advected, inverses, panels, predicted, filtered, noise_var[None], end_smoothed[None])


def passed_along(value, axis, by):
    size = lax.axis_size(axis)
    return lax.ppermute(value, axis, [(i, (i + by) % size) for i in range(size)])


def per_device(filtered, panels, tiles, neighbours, noise_var, end_smoothed):
    steps_here, cells_here, rank_width = panels.shape
    blocks_here = tiles.shape[0]
    block_cells = tiles.shape[2]
    cell_devices = lax.axis_size("cells")
    time_devices = lax.axis_size("tm")
    block_total = blocks_here * cell_devices
    window_first = (lax.axis_index("cells") - 2) * blocks_here
    position = jnp.mod(neighbours - window_first, block_total)
    rounded_means = filtered.astype(jnp.bfloat16)
    pieces = {0: (panels, rounded_means)}
    for heading in (-1, 1):
        for hops in (1, 2):
            pieces[hops * heading] = passed_along((panels, rounded_means), "cells", -heading * hops)
    window_panels = jnp.concatenate(
        [
            pieces[offset][0].reshape(steps_here, blocks_here, block_cells, rank_width)
            for offset in (-2, -1, 0, 1, 2)
        ],
        axis=1,
    )
    window_means = jnp.concatenate(
        [
            pieces[offset][1].reshape(steps_here, blocks_here, block_cells)
            for offset in (-2, -1, 0, 1, 2)
        ],
        axis=1,
    )
    advected = jnp.einsum(
        "rkij,trkjc->tric", tiles, window_panels[:, position], preferred_element_type=jnp.float32
    ).reshape(steps_here, cells_here, rank_width)
    predicted_state = jnp.einsum(
        "rkij,trkj->tri", tiles, window_means[:, position], preferred_element_type=jnp.float32
    ).reshape(steps_here, cells_here)
    system = summed_system(advected, noise_var, cell_devices)
    inverses = jnp.stack([inverse(system[t]) for t in range(steps_here)])
    return sweep_back(
        advected, inverses, panels, predicted_state, filtered, noise_var, end_smoothed, cell_devices, time_devices
    )


def solution(mesh):
    placed = (
        P("tm", "cells"),
        P("tm", "cells", None),
        P("cells", None, None, None),
        P("cells", None),
        P("cells"),
        P("cells"),
    )
    return jax.shard_map(
        per_device, mesh=mesh, in_specs=placed, out_specs=P("tm", "cells"), check_vma=False
    )
```

time: 402 us -> 129 us (0.32); the launches traced: 395 us -> 129 us
  other arithmetic: 140 us -> 2.16 us
  Pallas kernels: 0 us -> 67.9 us
  blocking collectives: 64.1 us -> 0 us
  waiting for transfers between devices: 68.2 us -> 20.5 us
  matrix products: 51.3 us -> 5.44 us
  local copies, waits for them, and re-layouts: 35.3 us -> 17.1 us
  between operations: 16.7 us -> 0.11 us
  starting transfers between devices: 19.9 us -> 15.7 us
    another operation x18 -> x0, other arithmetic: 131 us -> none  [the longest x14 87.7 us: per_device(): factor_list = [jnp.linalg.cholesky(system[0])]]
    pallas_call x0 -> x3, Pallas kernels: none -> 67.9 us  [the longest x1 24.2 us: summed_system(): pl.pallas_call(functools.partial(gram_kernel, n), out_shape=jax.ShapeDtyp...]
    psum x2 -> x0, blocking collectives: 64.1 us -> none  [project_onto_rank(): lax.psum(jnp.dot(vector, scaled_rows, precision=maximal_precision), 'cells')]
    psum x1 -> x0, waiting for transfers between devices: 58.8 us -> none  [per_device(): summed = lax.psum(local_gram, 'cells')]
    another operation x34 -> x0, matrix products: 39.5 us -> none  [the longest x14 15 us: cholesky_apply(): lax.linalg.triangular_solve(factor, halfway, left_side=True, lower=True,...]
    another operation x18 -> x1, local copies, waits for them, and re-layouts: 16.6 us -> 0.02 us  [the longest x13 14.8 us: cholesky_apply(): lax.linalg.triangular_solve(factor, halfway, left_side=True, lower=True,...]
    ppermute x8, waiting for transfers between devices: 5.23 us -> 20.5 us  [passed_along(): lax.ppermute(value, axis, [(i, (i + by) % size) for i in range(size)])]
    dot_general x5 -> x0, matrix products: 7.37 us -> none  [the longest x2 3.18 us: sweep(): jnp.dot(panels[step_lookup].astype(jnp.float32), coefficient, precision=m...]
  transfers between devices with their start and end apart: 10 -> 8, of which waited for: 5 -> 4; matrix products, arithmetic and copies ran while one was open for 3% -> 8% of each run, Pallas kernels for 0% -> 0%
where the time goes in v1:
time: 129 us
  Pallas kernels  67.9 us (53%)
  waiting for transfers between devices  20.5 us (16%)
  local copies, waits for them, and re-layouts  17.1 us (13%)
  starting transfers between devices  15.7 us (12%)
  matrix products  5.44 us (4%)
  other arithmetic  2.16 us (2%)
    pallas_call x1, Pallas kernels, summed_system(): pl.pallas_call(functools.partial(gram_kernel, n), out_shape=jax.ShapeDtyp...  24.2 us
    pallas_call x1, Pallas kernels, inverse(): pl.pallas_call(inverse_kernel, out_shape=jax.ShapeDtypeStruct((r, r), jnp...  23 us
    pallas_call x1, Pallas kernels, sweep_back(): pl.pallas_call(functools.partial(sweep_kernel, n, sections), out_shape=ja...  20.7 us
    ppermute x8, waiting for transfers between devices, passed_along(): lax.ppermute(value, axis, [(i, (i + by) % size) for i in range(size)])  20.5 us
    ppermute x8, starting transfers between devices, passed_along(): lax.ppermute(value, axis, [(i, (i + by) % size) for i in range(size)])  15.7 us
    unnamed x20, local copies, waits for them, and re-layouts  7.27 us
    gather x1, local copies, waits for them, and re-layouts, per_device(): window_panels[:, position]  5.61 us
    dot_general x1, matrix products, per_device(): jnp.einsum('rkij,trkjc->tric', tiles, window_panels[:, position], preferr...  4.73 us
  transfers between devices with their start and end apart: 8, of which 4 were waited for; matrix products, arithmetic and copies ran while one was open for 8% of the time, Pallas kernels for 0%

profile of v1, /device:TPU:0, one launch (start us, length us, event | category | flops | bytes accessed | tf_op | source)
XLA Modules:
  0.0 128.9 jit_solution(17087885614528277928)
XLA Ops:
  0.0 0.0 copy-start
  0.0 0.0 copy-start.3
  0.0 3.0 %collective-permute-start = (bf16[1,512,512]{2,1,0:T(8,128)(2,1)}, bf16[1,512,512]{2,1,0:T(8,128)(2,1)}, u32[]{:S(2)}, u32[]{:S(2)}) collective-permute-start(bf16[1,512,512]{2,1,0:T(8,128)(2,1)} %pan_ref.1), channel_id=1, source_target_pairs={{0,2},{1,3},{2,4},{3,5},{4,6},{5,7},{6,8},{7,9},{8,10},{9,11},{10,... | collective-permute-start | bytes 1572872 | tf_op jit(solution)/shard_map/ppermute | solution.py:313
  3.0 0.0 collective-permute-start.1
  3.0 0.7 convert_element_type.3
  3.7 1.5 %collective-permute-start.4 = (bf16[1,512]{1,0:T(2,128)(2,1)S(1)}, bf16[1,512]{1,0:T(2,128)(2,1)S(1)}, u32[]{:S(2)}, u32[]{:S(2)}) collective-permute-start(bf16[1,512]{1,0:T(2,128)(2,1)S(1)} %convert_element_type.3), channel_id=1, source_target_pairs={{0,2},{1,3},{2,4},{3,5},{4,6},{5,7},{6,8},{7,9},{8,10},{9,11},{10,... | collective-permute-start | bytes 3080 | tf_op jit(solution)/shard_map/ppermute | solution.py:313
  5.2 1.4 %collective-permute-start.5 = (bf16[1,512]{1,0:T(2,128)(2,1)S(1)}, bf16[1,512]{1,0:T(2,128)(2,1)S(1)}, u32[]{:S(2)}, u32[]{:S(2)}) collective-permute-start(bf16[1,512]{1,0:T(2,128)(2,1)S(1)} %convert_element_type.3), channel_id=1, source_target_pairs={{0,1},{1,2},{2,3},{3,4},{4,5},{5,6},{6,7},{7,8},{8,9},{9,10},{10,1... | collective-permute-start | bytes 3080 | tf_op jit(solution)/shard_map/ppermute | solution.py:313
  6.6 3.1 %collective-permute-start.6 = (bf16[1,512]{1,0:T(2,128)(2,1)S(1)}, bf16[1,512]{1,0:T(2,128)(2,1)S(1)}, u32[]{:S(2)}, u32[]{:S(2)}) collective-permute-start(bf16[1,512]{1,0:T(2,128)(2,1)S(1)} %convert_element_type.3), channel_id=1, source_target_pairs={{0,15},{1,0},{2,1},{3,2},{4,3},{5,4},{6,5},{7,6},{8,7},{9,8},{10,9... | collective-permute-start | bytes 3080 | tf_op jit(solution)/shard_map/ppermute | solution.py:313
  9.7 0.7 compare_select_fusion
  10.3 0.7 convert_reduce_fusion
  11.0 0.1 reshape.59
  11.1 8.1 %collective-permute-done.4 = bf16[1,512]{1,0:T(2,128)(2,1)S(1)} collective-permute-done((bf16[1,512]{1,0:T(2,128)(2,1)S(1)}, bf16[1,512]{1,0:T(2,128)(2,1)S(1)}, u32[]{:S(2)}, u32[]{:S(2)}) %collective-permute-start.4) | collective-permute-done | bytes 1056 | tf_op jit(solution)/shard_map/ppermute | solution.py:313
  19.2 2.0 %collective-permute-start.7 = (bf16[1,512]{1,0:T(2,128)(2,1)S(1)}, bf16[1,512]{1,0:T(2,128)(2,1)S(1)}, u32[]{:S(2)}, u32[]{:S(2)}) collective-permute-start(bf16[1,512]{1,0:T(2,128)(2,1)S(1)} %convert_element_type.3), channel_id=1, source_target_pairs={{0,14},{1,15},{2,0},{3,1},{4,2},{5,3},{6,4},{7,5},{8,6},{9,7},{10,... | collective-permute-start | bytes 3080 | tf_op jit(solution)/shard_map/ppermute | solution.py:313
  21.2 1.5 %copy.7.noise_ref = f32[512,1]{1,0:T(8,128)} copy(f32[512,1]{0,1:T(1,128)} %bitcast.35) | data formatting | bytes 4096 | tf_op jit(solution)/shard_map/broadcast_in_dim | solution.py:210
  22.8 1.2 collective-permute-done.5
  23.9 4.1 %collective-permute-start.2 = (bf16[1,512,512]{2,1,0:T(8,128)(2,1)}, bf16[1,512,512]{2,1,0:T(8,128)(2,1)}, u32[]{:S(2)}, u32[]{:S(2)}) collective-permute-start(bf16[1,512,512]{2,1,0:T(8,128)(2,1)} %pan_ref.1), channel_id=1, source_target_pairs={{0,15},{1,0},{2,1},{3,2},{4,3},{5,4},{6,5},{7,6},{8,7},{9,8},{10,9... | collective-permute-start | bytes 1572872 | tf_op jit(solution)/shard_map/ppermute | solution.py:313
  28.1 0.0 collective-permute-done.6
  28.1 0.6 collective-permute-start.3
  28.7 0.0 collective-permute-done.7
  28.8 0.6 gather_fusion.1
  29.4 0.0 copy-done
  29.4 0.7 fusion.1
  30.2 0.0 collective-permute-done
  30.2 1.9 %constant_dynamic-update-slice_fusion.4 = bf16[1,10,256,512]{3,2,1,0:T(8,128)(2,1)} fusion(bf16[1,2,256,512]{3,2,1,0:T(8,128)(2,1)} %bitcast), kind=kLoop, calls=%fused_computation.6 | loop fusion | bytes 1048576
  32.1 0.0 collective-permute-done.1
  32.1 0.8 constant_dynamic-update-slice_fusion.3
  32.9 0.0 copy-done.3
  32.9 0.8 constant_dynamic-update-slice_fusion.2
  33.8 6.5 %collective-permute-done.2 = bf16[1,512,512]{2,1,0:T(8,128)(2,1)} collective-permute-done((bf16[1,512,512]{2,1,0:T(8,128)(2,1)}, bf16[1,512,512]{2,1,0:T(8,128)(2,1)}, u32[]{:S(2)}, u32[]{:S(2)}) %collective-permute-start.2) | collective-permute-done | bytes 524320 | tf_op jit(solution)/shard_map/ppermute | solution.py:313
  40.2 1.9 %constant_dynamic-update-slice_fusion.1 = bf16[1,10,256,512]{3,2,1,0:T(8,128)(2,1)} fusion(bf16[1,10,256,512]{3,2,1,0:T(8,128)(2,1)} %constant_dynamic-update-slice_fusion.2, bf16[1,2,256,512]{3,2,1,0:T(8,128)(2,1)} %bitcast.3), kind=kLoop, calls=%fused_computation.3 | loop fusion | bytes 1048576
  42.1 4.8 %collective-permute-done.3 = bf16[1,512,512]{2,1,0:T(8,128)(2,1)} collective-permute-done((bf16[1,512,512]{2,1,0:T(8,128)(2,1)}, bf16[1,512,512]{2,1,0:T(8,128)(2,1)}, u32[]{:S(2)}, u32[]{:S(2)}) %collective-permute-start.3) | collective-permute-done | bytes 524320 | tf_op jit(solution)/shard_map/ppermute | solution.py:313
  46.9 1.9 %constant_dynamic-update-slice_fusion = bf16[1,10,256,512]{3,2,1,0:T(8,128)(2,1)} fusion(bf16[1,10,256,512]{3,2,1,0:T(8,128)(2,1)} %constant_dynamic-update-slice_fusion.1, bf16[1,2,256,512]{3,2,1,0:T(8,128)(2,1)} %bitcast.4), kind=kLoop, calls=%fused_computation.2 | loop fusion | bytes 1048576 | tf_op jit(solution)/shard_map/concatenate | solution.py:330
  48.8 5.6 %gather_fusion = bf16[18,256,512]{2,1,0:T(8,128)(2,1)} fusion(bf16[10,256,512]{2,1,0:T(8,128)(2,1)} %bitcast.5, s32[1024]{0:T(1024)S(1)} %pad_clamp_fusion), kind=kCustom, calls=%fused_computation | custom fusion | bytes 9437256 | tf_op jit(solution)/shard_map/gather | solution.py:345
  54.4 4.7 %fusion.2 = f32[2,512,256,1]{1,2,3,0:T(8,128)} fusion(bf16[2,9,256,256]{3,2,1,0:T(8,128)(2,1)S(1)} %copy-done, bf16[2,9,256,512]{3,2,1,0:T(8,128)(2,1)} %bitcast.39), kind=kOutput, calls=%fused_computation.16 | convolution fusion | flops 1207959552 | bytes 8126464 | tf_op jit(solution)/shard_map/rkij,trkjc->tric/dot_general | solution.py:344
  59.2 0.0 copy-start.1
  59.2 0.0 copy-start.4
  59.2 0.0 copy-start.5
  59.2 0.0 copy-start.6
  59.2 24.2 %shard_map.64 = f32[1,512,512]{2,1,0:T(8,128)} custom-call(f32[1,512,512]{2,1,0:T(8,128)} %bitcast.30, f32[512,1]{1,0:T(8,128)} %copy.7.noise_ref), custom_call_target="tpu_custom_call" | custom-call | tf_op jit(solution)/shard_map/pallas_call | solution.py:192
  83.4 0.0 copy-start.2
  83.4 1.2 copy-done.2
  84.6 23.0 %shard_map.65 = f32[512,512]{1,0:T(8,128)S(1)} custom-call(f32[512,512]{1,0:T(8,128)S(1)} %bitcast.33), custom_call_target="tpu_custom_call" | custom-call | tf_op jit(solution)/shard_map/pallas_call | solution.py:68
  107.6 0.0 copy-done.1
  107.6 0.0 copy-done.4
  107.6 0.0 copy-done.5
  107.6 0.0 copy-done.6
  107.6 20.7 %shard_map.66 = f32[1,512]{1,0:T(1,128)S(1)} custom-call(f32[1,512,512]{2,1,0:T(8,128)S(1)} %bitcast.31, f32[1,512,512]{2,1,0:T(8,128)S(1)} %bitcast.32, bf16[1,512,512]{2,1,0:T(8,128)(2,1)S(1)} %copy-done.3, f32[1,512]{1,0:T(1,128)S(1)} %bitcast.37, f32[1,512]{1,0:T(1,128)S(1)} %copy-done.4, f32[1,512]{1,0:T(1,128)S(1)} %bitcast.36, f32[1,512]{1,0:T(1,128)S(1)} %bitcast.38), custom_call_target="tpu_custom_call" | custom-call | tf_op jit(solution)/shard_map/pallas_call | solution.py:293
  128.3 0.6 copy.19
  (14 shorter events, 0.2 us)
Async XLA Ops:
  0.0 29.4 %copy-start = (bf16[2,9,256,256]{3,2,1,0:T(8,128)(2,1)S(1)}, bf16[2,9,256,256]{3,2,1,0:T(8,128)(2,1)}, u32[]{:S(2)}) copy-start(bf16[2,9,256,256]{3,2,1,0:T(8,128)(2,1)} %param.8) | copy-start | bytes 7077892
  0.0 32.9 %copy-start.3 = (bf16[1,512,512]{2,1,0:T(8,128)(2,1)S(1)}, bf16[1,512,512]{2,1,0:T(8,128)(2,1)}, u32[]{:S(2)}) copy-start(bf16[1,512,512]{2,1,0:T(8,128)(2,1)} %pan_ref.1) | copy-start | bytes 1572868
  0.0 30.2 %collective-permute-start = (bf16[1,512,512]{2,1,0:T(8,128)(2,1)}, bf16[1,512,512]{2,1,0:T(8,128)(2,1)}, u32[]{:S(2)}, u32[]{:S(2)}) collective-permute-start(bf16[1,512,512]{2,1,0:T(8,128)(2,1)} %pan_ref.1), channel_id=1, source_target_pairs={{0,2},{1,3},{2,4},{3,5},{4,6},{5,7},{6,8},{7,9},{8,10},{9,11},{10,... | collective-permute-start | bytes 1572872 | tf_op jit(solution)/shard_map/ppermute | solution.py:313
  3.0 29.1 %collective-permute-start.1 = (bf16[1,512,512]{2,1,0:T(8,128)(2,1)}, bf16[1,512,512]{2,1,0:T(8,128)(2,1)S(1)}, u32[]{:S(2)}, u32[]{:S(2)}) collective-permute-start(bf16[1,512,512]{2,1,0:T(8,128)(2,1)} %pan_ref.1), channel_id=1, source_target_pairs={{0,1},{1,2},{2,3},{3,4},{4,5},{5,6},{6,7},{7,8},{8,9},{9,10},{10,1... | collective-permute-start | bytes 1572872 | tf_op jit(solution)/shard_map/ppermute | solution.py:313
  3.7 15.5 %collective-permute-start.4 = (bf16[1,512]{1,0:T(2,128)(2,1)S(1)}, bf16[1,512]{1,0:T(2,128)(2,1)S(1)}, u32[]{:S(2)}, u32[]{:S(2)}) collective-permute-start(bf16[1,512]{1,0:T(2,128)(2,1)S(1)} %convert_element_type.3), channel_id=1, source_target_pairs={{0,2},{1,3},{2,4},{3,5},{4,6},{5,7},{6,8},{7,9},{8,10},{9,11},{10,... | collective-permute-start | bytes 3080 | tf_op jit(solution)/shard_map/ppermute | solution.py:313
  5.2 18.7 %collective-permute-start.5 = (bf16[1,512]{1,0:T(2,128)(2,1)S(1)}, bf16[1,512]{1,0:T(2,128)(2,1)S(1)}, u32[]{:S(2)}, u32[]{:S(2)}) collective-permute-start(bf16[1,512]{1,0:T(2,128)(2,1)S(1)} %convert_element_type.3), channel_id=1, source_target_pairs={{0,1},{1,2},{2,3},{3,4},{4,5},{5,6},{6,7},{7,8},{8,9},{9,10},{10,1... | collective-permute-start | bytes 3080 | tf_op jit(solution)/shard_map/ppermute | solution.py:313
  6.6 21.5 %collective-permute-start.6 = (bf16[1,512]{1,0:T(2,128)(2,1)S(1)}, bf16[1,512]{1,0:T(2,128)(2,1)S(1)}, u32[]{:S(2)}, u32[]{:S(2)}) collective-permute-start(bf16[1,512]{1,0:T(2,128)(2,1)S(1)} %convert_element_type.3), channel_id=1, source_target_pairs={{0,15},{1,0},{2,1},{3,2},{4,3},{5,4},{6,5},{7,6},{8,7},{9,8},{10,9... | collective-permute-start | bytes 3080 | tf_op jit(solution)/shard_map/ppermute | solution.py:313
  19.2 9.6 %collective-permute-start.7 = (bf16[1,512]{1,0:T(2,128)(2,1)S(1)}, bf16[1,512]{1,0:T(2,128)(2,1)S(1)}, u32[]{:S(2)}, u32[]{:S(2)}) collective-permute-start(bf16[1,512]{1,0:T(2,128)(2,1)S(1)} %convert_element_type.3), channel_id=1, source_target_pairs={{0,14},{1,15},{2,0},{3,1},{4,2},{5,3},{6,4},{7,5},{8,6},{9,7},{10,... | collective-permute-start | bytes 3080 | tf_op jit(solution)/shard_map/ppermute | solution.py:313
  23.9 16.3 %collective-permute-start.2 = (bf16[1,512,512]{2,1,0:T(8,128)(2,1)}, bf16[1,512,512]{2,1,0:T(8,128)(2,1)}, u32[]{:S(2)}, u32[]{:S(2)}) collective-permute-start(bf16[1,512,512]{2,1,0:T(8,128)(2,1)} %pan_ref.1), channel_id=1, source_target_pairs={{0,15},{1,0},{2,1},{3,2},{4,3},{5,4},{6,5},{7,6},{8,7},{9,8},{10,9... | collective-permute-start | bytes 1572872 | tf_op jit(solution)/shard_map/ppermute | solution.py:313
  28.1 18.8 %collective-permute-start.3 = (bf16[1,512,512]{2,1,0:T(8,128)(2,1)}, bf16[1,512,512]{2,1,0:T(8,128)(2,1)}, u32[]{:S(2)}, u32[]{:S(2)}) collective-permute-start(bf16[1,512,512]{2,1,0:T(8,128)(2,1)} %pan_ref.1), channel_id=1, source_target_pairs={{0,14},{1,15},{2,0},{3,1},{4,2},{5,3},{6,4},{7,5},{8,6},{9,7},{10,... | collective-permute-start | bytes 1572872 | tf_op jit(solution)/shard_map/ppermute | solution.py:313
  59.2 48.4 %copy-start.1 = (f32[2,512,256,1]{1,2,3,0:T(8,128)S(1)}, f32[2,512,256,1]{1,2,3,0:T(8,128)}, u32[]{:S(2)}) copy-start(f32[2,512,256,1]{1,2,3,0:T(8,128)} %fusion.2) | copy-start | bytes 3145732
  59.2 48.4 %copy-start.4 = (f32[1,512]{1,0:T(1,128)S(1)}, f32[1,512]{1,0:T(1,128)}, u32[]{:S(2)}) copy-start(f32[1,512]{1,0:T(1,128)} %filt_ref.1) | copy-start | bytes 6148
  59.2 48.4 %copy-start.5 = (f32[512]{0:T(512)S(1)}, f32[512]{0:T(512)}, u32[]{:S(2)}) copy-start(f32[512]{0:T(512)} %param.10) | copy-start | bytes 6148
  59.2 48.4 %copy-start.6 = (f32[512]{0:T(512)S(1)}, f32[512]{0:T(512)}, u32[]{:S(2)}) copy-start(f32[512]{0:T(512)} %param.11) | copy-start | bytes 6148
  83.4 1.2 copy-start.2

commit v2 on v1

--- a/solution.py
+++ b/solution.py
@@ -75,9 +75,14 @@
     return [[p for p in range(count // 2) if p % 2 == half] for half in (0, 1)]
 
 
-def gram_kernel(n, adv_ref, noise_ref, out_ref, scaled, packed, landed, parts, slots, reduced, gathered, other, sems, sems_chip):
+def gram_kernel(n, pan_ref, filt_ref, tiles_ref, near_ref, noise_ref, out_ref, adv_ref, pred_ref,
+                window, means, tiles, dense, scaled, packed, landed, parts, slots, reduced, gathered, other,
+                sems, sems_chip, sems_halo, sems_mean, sem_tiles):
     me = lax.axis_index("cells")
     steps, cells, rank = adv_ref.shape
+    blocks, per_row, size = tiles.shape[:3]
+    wide = window.shape[-1]
+    chunks = rank // wide
     count = rank // B
     pairs = block_pairs(rank)
     chips = n // 2
@@ -85,31 +90,117 @@
     partner = chip * 2 + (1 - core)
     rows = packed.shape[2] // steps
 
+    fetch = pltpu.make_async_copy(tiles_ref, tiles, sem_tiles)
+    fetch.start()
     barrier = pltpu.get_barrier_semaphore()
     for k in range(1, n):
         pl.semaphore_signal(barrier, inc=1, device_id={"cells": (me + k) % n}, device_id_type=MESH)
-
+    pl.semaphore_wait(barrier, n - 1)
+
+    def mean_copy(offset):
+        return pltpu.make_async_remote_copy(
+            filt_ref, means.at[2 - offset], sems_mean.at[0, 2 - offset], sems_mean.at[1, 2 - offset],
+            device_id={"cells": (me + offset + n) % n}, device_id_type=MESH,
+        )
+
+    def own_chunk(j):
+        return pan_ref.at[:, :, j * wide : (j + 1) * wide]
+
+    def near(j):
+        return pltpu.make_async_remote_copy(
+            own_chunk(j), window.at[1 + 2 * core, j], sems_halo.at[0, 0, j], sems_halo.at[1, 0, j],
+            device_id={"cells": partner}, device_id_type=MESH,
+        )
+
+    def far(j, s):
+        return pltpu.make_async_remote_copy(
+            own_chunk(j), window.at[4 * s, j], sems_halo.at[0, 1 + s, j], sems_halo.at[1, 1 + s, j],
+            device_id={"cells": (me + 2 - 4 * s + n) % n}, device_id_type=MESH,
+        )
+
+    def forward(j):
+        return pltpu.make_async_remote_copy(
+            window.at[4 - 4 * core, j], window.at[3 - 2 * core, j],
+            sems_halo.at[0, 3, j], sems_halo.at[1, 3, j],
+            device_id={"cells": partner}, device_id_type=MESH,
+        )
+
+    for offset in (1, -1, 2, -2):
+        mean_copy(offset).start()
+    for j in range(chunks):
+        far(j, 0).start()
+        far(j, 1).start()
+        near(j).start()
+
+    fetch.wait()
+    first_block = (me - 2) * blocks
+    total_blocks = n * blocks
+    for b in range(blocks):
+        places = [(near_ref[b, k] - first_block + total_blocks) % total_blocks for k in range(per_row)]
+        for w in range(5 * blocks):
+            at = jnp.int32(0)
+            found = jnp.int32(0)
+            for k in range(per_row):
+                hit = (places[k] == w).astype(jnp.int32)
+                at = jnp.maximum(at, hit * k)
+                found = jnp.maximum(found, hit)
+            keep = jnp.full((size, size), found, jnp.int32) > 0
+            tile = tiles[b, at].astype(jnp.float32)
+            dense[b * size : (b + 1) * size, w * size : (w + 1) * size] = jnp.where(keep, tile, 0.0).astype(jnp.bfloat16)
+
+    for offset in (1, -1, 2, -2):
+        mean_copy(offset).wait()
     for t in range(steps):
-        scaled[...] = adv_ref[t] / noise_ref[...]
-        for half in (0, 1):
-            for at, p in enumerate(pairs[half]):
-                long, short = count - 1 - p, p
-                pieces = []
-                for r in (long, short):
-                    pieces.append(
-                        lax.dot_general(
-                            scaled[:, r * B : (r + 1) * B],
-                            adv_ref[t, :, : (r + 1) * B],
-                            (((0,), (0,)), ((), ())),
-                            precision=HI,
-                            preferred_element_type=jnp.float32,
-                        )
-                    )
-                value = jnp.concatenate(pieces, axis=1)
-                per = B * len(pairs[half]) // chips
+        total = jnp.zeros((1, cells), jnp.float32)
+        for s in range(5):
+            row = filt_ref[t : t + 1] if s == 2 else means[s, t : t + 1]
+            total = total + lax.dot_general(
+                row.astype(jnp.bfloat16), dense[:, s * cells : (s + 1) * cells],
+                (((1,), (1,)), ((), ())), preferred_element_type=jnp.float32,
+            )
+        pred_ref[t : t + 1] = total
+
+    home = {}
+    for half in (0, 1):
+        for at, p in enumerate(pairs[half]):
+            long, short = count - 1 - p, p
+            home[long] = (half, at, 0)
+            home[short] = (half, at, (long + 1) * B)
+    per = rows
+    for j in range(chunks):
+        here = slice(j * wide, (j + 1) * wide)
+        far(j, 1 - core).wait_recv()
+        forward(j).start()
+        near(j).wait_recv()
+        far(j, core).wait_recv()
+        forward(j).wait_recv()
+        for t in range(steps):
+            product = jnp.zeros((cells, wide), jnp.float32)
+            for s in range(5):
+                piece = pan_ref[t, :, here] if s == 2 else window[s, j, t]
+                product = product + jnp.dot(
+                    dense[:, s * cells : (s + 1) * cells], piece, preferred_element_type=jnp.float32
+                )
+            adv_ref[t, :, here] = product
+            scaled[t, :, here] = product / noise_ref[...]
+            for r in range(j * wide // B, (j + 1) * wide // B):
+                value = lax.dot_general(
+                    scaled[t, :, r * B : (r + 1) * B],
+                    adv_ref[t, :, : (r + 1) * B],
+                    (((0,), (0,)), ((), ())),
+                    precision=HI,
+                    preferred_element_type=jnp.float32,
+                )
+                half, at, begin = home[r]
                 for q in range(B // per):
-                    packed[half, at * (B // per) + q, t * rows : t * rows + per] = value[q * per : (q + 1) * per]
-    pl.semaphore_wait(barrier, n - 1)
+                    packed[half, at * (B // per) + q, t * rows : (t + 1) * rows, begin : begin + (r + 1) * B] = value[
+                        q * per : (q + 1) * per
+                    ]
+    for j in range(chunks):
+        near(j).wait_send()
+        far(j, 0).wait_send()
+        far(j, 1).wait_send()
+        forward(j).wait_send()
 
     first = pltpu.make_async_remote_copy(
         packed.at[1 - core], landed, sems.at[0], sems.at[1], device_id={"cells": partner}, device_id_type=MESH
@@ -182,20 +273,30 @@
         unpack(0, other)
 
 
-def summed_system(advected, noise_var, n):
-    steps, cells, rank = advected.shape
+def summed_system(panels, filtered, tiles, neighbours, noise_var, n):
+    steps, cells, rank = panels.shape
     chips = n // 2
     per_half = (rank // B) // 4
     rows = B * per_half // chips * steps
     wide = rank + B
+    chunk = 2 * B
     f32 = jnp.float32
+    vmem = pl.BlockSpec(memory_space=pltpu.VMEM)
     return pl.pallas_call(
         functools.partial(gram_kernel, n),
-        out_shape=jax.ShapeDtypeStruct((steps, rank, rank), f32),
-        in_specs=[pl.BlockSpec(memory_space=pltpu.VMEM)] * 2,
-        out_specs=pl.BlockSpec(memory_space=pltpu.VMEM),
+        out_shape=(
+            jax.ShapeDtypeStruct((steps, rank, rank), f32),
+            jax.ShapeDtypeStruct((steps, cells, rank), f32),
+            jax.ShapeDtypeStruct((steps, cells), f32),
+        ),
+        in_specs=[vmem, vmem, pl.BlockSpec(memory_space=pl.ANY), pl.BlockSpec(memory_space=pltpu.SMEM), vmem],
+        out_specs=[vmem] * 3,
         scratch_shapes=[
-            pltpu.VMEM((cells, rank), f32),
+            pltpu.VMEM((5, rank // chunk, steps, cells, chunk), panels.dtype),
+            pltpu.VMEM((5, steps, cells), f32),
+            pltpu.VMEM(tiles.shape, tiles.dtype),
+            pltpu.VMEM((cells, 5 * cells), tiles.dtype),
+            pltpu.VMEM((steps, cells, rank), f32),
             pltpu.VMEM((2, chips, rows, wide), f32),
             pltpu.VMEM((chips, rows, wide), f32),
             pltpu.VMEM((chips, rows, wide), f32),
@@ -205,9 +306,12 @@
             pltpu.VMEM((chips, rows, wide), f32),
             pltpu.SemaphoreType.DMA((4,)),
             pltpu.SemaphoreType.DMA((4, chips)),
+            pltpu.SemaphoreType.DMA((2, 4, rank // chunk)),
+            pltpu.SemaphoreType.DMA((2, 5)),
+            pltpu.SemaphoreType.DMA,
         ],
         compiler_params=pltpu.CompilerParams(collective_id=0, has_side_effects=True, vmem_limit_bytes=56 << 20),
-    )(advected, noise_var[:, None])
+    )(panels, filtered, tiles, neighbours, noise_var[:, None])
 
 
 def split3(v):
@@ -308,49 +412,12 @@
     )(advected, inverses, panels, predicted, filtered, noise_var[None], end_smoothed[None])
 
 
-def passed_along(value, axis, by):
-    size = lax.axis_size(axis)
-    return lax.ppermute(value, axis, [(i, (i + by) % size) for i in range(size)])
-
-
 def per_device(filtered, panels, tiles, neighbours, noise_var, end_smoothed):
-    steps_here, cells_here, rank_width = panels.shape
-    blocks_here = tiles.shape[0]
-    block_cells = tiles.shape[2]
     cell_devices = lax.axis_size("cells")
-    time_devices = lax.axis_size("tm")
-    block_total = blocks_here * cell_devices
-    window_first = (lax.axis_index("cells") - 2) * blocks_here
-    position = jnp.mod(neighbours - window_first, block_total)
-    rounded_means = filtered.astype(jnp.bfloat16)
-    pieces = {0: (panels, rounded_means)}
-    for heading in (-1, 1):
-        for hops in (1, 2):
-            pieces[hops * heading] = passed_along((panels, rounded_means), "cells", -heading * hops)
-    window_panels = jnp.concatenate(
-        [
-            pieces[offset][0].reshape(steps_here, blocks_here, block_cells, rank_width)
-            for offset in (-2, -1, 0, 1, 2)
-        ],
-        axis=1,
-    )
-    window_means = jnp.concatenate(
-        [
-            pieces[offset][1].reshape(steps_here, blocks_here, block_cells)
-            for offset in (-2, -1, 0, 1, 2)
-        ],
-        axis=1,
-    )
-    advected = jnp.einsum(
-        "rkij,trkjc->tric", tiles, window_panels[:, position], preferred_element_type=jnp.float32
-    ).reshape(steps_here, cells_here, rank_width)
-    predicted_state = jnp.einsum(
-        "rkij,trkj->tri", tiles, window_means[:, position], preferred_element_type=jnp.float32
-    ).reshape(steps_here, cells_here)
-    system = summed_system(advected, noise_var, cell_devices)
-    inverses = jnp.stack([inverse(system[t]) for t in range(steps_here)])
+    system, advected, predicted = summed_system(panels, filtered, tiles, neighbours, noise_var, cell_devices)
+    inverses = jnp.stack([inverse(system[t]) for t in range(panels.shape[0])])
     return sweep_back(
-        advected, inverses, panels, predicted_state, filtered, noise_var, end_smoothed, cell_devices, time_devices
+        advected, inverses, panels, predicted, filtered, noise_var, end_smoothed, cell_devices, lax.axis_size("tm")
     )
 
 

time: 129 us -> 103 us (0.80)
  Pallas kernels: 67.9 us -> 98.4 us
  waiting for transfers between devices: 20.5 us -> 0 us
  starting transfers between devices: 15.7 us -> 0 us
  local copies, waits for them, and re-layouts: 17.1 us -> 4.09 us
  matrix products: 5.44 us -> 0 us
  other arithmetic: 2.16 us -> 0 us
    pallas_call x1, Pallas kernels: 24.2 us -> 54.8 us  [summed_system(): pl.pallas_call(functools.partial(gram_kernel, n), out_shape=(jax.ShapeDty...]
    ppermute x8 -> x0, waiting for transfers between devices: 20.5 us -> none  [passed_along(): lax.ppermute(value, axis, [(i, (i + by) % size) for i in range(size)])]
    ppermute x8 -> x0, starting transfers between devices: 15.7 us -> none  [passed_along(): lax.ppermute(value, axis, [(i, (i + by) % size) for i in range(size)])]
    gather x2 -> x0, local copies, waits for them, and re-layouts: 6.21 us -> none  [the longest x1 5.61 us: per_device(): window_panels[:, position]]
    dot_general x2 -> x0, matrix products: 5.44 us -> none  [the longest x1 4.73 us: per_device(): jnp.einsum('rkij,trkjc->tric', tiles, window_panels[:, position], preferr...]
    unnamed x20 -> x15, local copies, waits for them, and re-layouts: 7.27 us -> 2.57 us
    concatenate x2 -> x0, local copies, waits for them, and re-layouts: 1.93 us -> none  [the longest x1 1.89 us: per_device(): jnp.concatenate([pieces[offset][0].reshape(steps_here, blocks_here, block...]
    convert_element_type x2 -> x0, other arithmetic: 1.38 us -> none  [per_device(): rounded_means = filtered.astype(jnp.bfloat16)]
  transfers between devices with their start and end apart: 8 -> 0, of which waited for: 4 -> 0; matrix products, arithmetic and copies ran while one was open for 8% -> 0% of each run, Pallas kernels for 0% -> 0%
where the time goes in v2:
time: 103 us
  Pallas kernels  98.4 us (96%)
  local copies, waits for them, and re-layouts  4.09 us (4%)
    pallas_call x1, Pallas kernels, summed_system(): pl.pallas_call(functools.partial(gram_kernel, n), out_shape=(jax.ShapeDty...  54.8 us
    pallas_call x1, Pallas kernels, inverse(): pl.pallas_call(inverse_kernel, out_shape=jax.ShapeDtypeStruct((r, r), jnp...  23 us
    pallas_call x1, Pallas kernels, sweep_back(): pl.pallas_call(functools.partial(sweep_kernel, n, sections), out_shape=ja...  20.6 us
    unnamed x15, local copies, waits for them, and re-layouts  2.57 us

profile of v2, /device:TPU:0, one launch (start us, length us, event | category | flops | bytes accessed | tf_op | source)
XLA Modules:
  0.0 102.6 jit_solution(17399201439081835356)
XLA Ops:
  0.0 1.5 %copy.7.noise_ref = f32[512,1]{1,0:T(8,128)} copy(f32[512,1]{0,1:T(1,128)} %bitcast.7) | data formatting | bytes 4096 | tf_op jit(solution)/shard_map/broadcast_in_dim | solution.py:314
  1.5 0.0 copy-start
  1.5 0.0 copy-start.3
  1.5 0.0 copy-start.4
  1.5 0.0 copy-start.5
  1.5 54.8 %shard_map.64 = (f32[1,512,512]{2,1,0:T(8,128)}, f32[1,512,512]{2,1,0:T(8,128)}, f32[1,512]{1,0:T(1,128)}) custom-call(bf16[1,512,512]{2,1,0:T(8,128)(2,1)} %pan_ref.3, f32[1,512]{1,0:T(1,128)} %filt_ref.3, bf16[2,9,256,256]{3,2,1,0:T(8,128)(2,1)} %tiles_ref.1, s32[2,9]{1,0:T(2,128)} %near_ref.1, f32[512,1]{1,0:T(8,128)} %copy.7.noise_ref), custom_call_target="tpu_custom_call" | custom-call | tf_op jit(solution)/shard_map/pallas_call | solution.py:285
  56.4 0.0 copy-start.1
  56.4 0.0 copy-start.2
  56.4 1.3 %copy-done.2 = f32[1,512,512]{2,1,0:T(8,128)S(1)} copy-done((f32[1,512,512]{2,1,0:T(8,128)S(1)}, f32[1,512,512]{2,1,0:T(8,128)}, u32[]{:S(2)}) %copy-start.2) | copy-done | bytes 1048600
  57.7 23.0 %shard_map.65 = f32[512,512]{1,0:T(8,128)S(1)} custom-call(f32[512,512]{1,0:T(8,128)S(1)} %bitcast.6), custom_call_target="tpu_custom_call" | custom-call | tf_op jit(solution)/shard_map/pallas_call | solution.py:68
  80.7 0.0 copy-done
  80.7 0.0 copy-done.3
  80.7 0.0 copy-done.4
  80.7 0.0 copy-done.5
  80.7 0.0 copy-done.1
  80.7 0.0 copy-start.6
  80.7 0.7 copy-done.6
  81.4 20.6 %shard_map.66 = f32[1,512]{1,0:T(1,128)S(1)} custom-call(f32[1,512,512]{2,1,0:T(8,128)S(1)} %copy-done.1, f32[1,512,512]{2,1,0:T(8,128)S(1)} %bitcast.5, bf16[1,512,512]{2,1,0:T(8,128)(2,1)S(1)} %copy-done, f32[1,512]{1,0:T(1,128)S(1)} %copy-done.6, f32[1,512]{1,0:T(1,128)S(1)} %copy-done.3, f32[1,512]{1,0:T(1,128)S(1)} %bitcast.8, f32[1,512]{1,0:T(1,128)S(1)} %bitcast.9), custom_call_target="tpu_custom_call" | custom-call | tf_op jit(solution)/shard_map/pallas_call | solution.py:397
  102.0 0.6 copy.9
Async XLA Ops:
  1.5 79.2 %copy-start = (bf16[1,512,512]{2,1,0:T(8,128)(2,1)S(1)}, bf16[1,512,512]{2,1,0:T(8,128)(2,1)}, u32[]{:S(2)}) copy-start(bf16[1,512,512]{2,1,0:T(8,128)(2,1)} %pan_ref.3) | copy-start | bytes 1572868
  1.5 79.2 %copy-start.3 = (f32[1,512]{1,0:T(1,128)S(1)}, f32[1,512]{1,0:T(1,128)}, u32[]{:S(2)}) copy-start(f32[1,512]{1,0:T(1,128)} %filt_ref.3) | copy-start | bytes 6148
  1.5 79.2 %copy-start.4 = (f32[512]{0:T(512)S(1)}, f32[512]{0:T(512)}, u32[]{:S(2)}) copy-start(f32[512]{0:T(512)} %param.10) | copy-start | bytes 6148
  1.5 79.2 %copy-start.5 = (f32[512]{0:T(512)S(1)}, f32[512]{0:T(512)}, u32[]{:S(2)}) copy-start(f32[512]{0:T(512)} %param.11) | copy-start | bytes 6148
  56.4 24.3 %copy-start.1 = (f32[1,512,512]{2,1,0:T(8,128)S(1)}, f32[1,512,512]{2,1,0:T(8,128)}, u32[]{:S(2)}) copy-start(f32[1,512,512]{2,1,0:T(8,128)} %get-tuple-element.8.adv_ref) | copy-start | bytes 3145732
  56.4 1.3 %copy-start.2 = (f32[1,512,512]{2,1,0:T(8,128)S(1)}, f32[1,512,512]{2,1,0:T(8,128)}, u32[]{:S(2)}) copy-start(f32[1,512,512]{2,1,0:T(8,128)} %get-tuple-element.9) | copy-start | bytes 3145732
  80.7 0.7 copy-start.6

commit v3 on v2

--- a/solution.py
+++ b/solution.py
@@ -44,7 +44,7 @@
         rows[g] = lead
     return jnp.concatenate(rows, axis=0)
 
-def inverse_kernel(s_ref, o_ref, w_ref):
+def invert_into(s_ref, o_ref, w_ref):
     rank = s_ref.shape[-1]
     n = 128
     o_ref[...] = s_ref[...]
@@ -63,12 +63,6 @@
         return 0
     lax.fori_loop(0, rank // n, step, 0)
 
-def inverse(s):
-    r = s.shape[-1]
-    return pl.pallas_call(inverse_kernel, out_shape=jax.ShapeDtypeStruct((r, r), jnp.float32),
-        in_specs=[pl.BlockSpec(memory_space=pltpu.VMEM)], out_specs=pl.BlockSpec(memory_space=pltpu.VMEM),
-        scratch_shapes=[pltpu.VMEM((128, r), jnp.float32)],
-        compiler_params=pltpu.CompilerParams(vmem_limit_bytes=40 << 20))(s)
 
 def block_pairs(rank):
     count = rank // B
@@ -76,7 +70,7 @@
 
 
 def gram_kernel(n, pan_ref, filt_ref, tiles_ref, near_ref, noise_ref, out_ref, adv_ref, pred_ref,
-                window, means, tiles, dense, scaled, packed, landed, parts, slots, reduced, gathered, other,
+                window, means, tiles, dense, divisor, scaled, packed, landed, parts, slots, reduced, gathered, other,
                 sems, sems_chip, sems_halo, sems_mean, sem_tiles):
     me = lax.axis_index("cells")
     steps, cells, rank = adv_ref.shape
@@ -132,6 +126,7 @@
         far(j, 1).start()
         near(j).start()
 
+    divisor[...] = jnp.broadcast_to(noise_ref[...], (B, cells)).T
     fetch.wait()
     first_block = (me - 2) * blocks
     total_blocks = n * blocks
@@ -182,7 +177,7 @@
                     dense[:, s * cells : (s + 1) * cells], piece, preferred_element_type=jnp.float32
                 )
             adv_ref[t, :, here] = product
-            scaled[t, :, here] = product / noise_ref[...]
+            scaled[t, :, here] = product / divisor[:, :1]
             for r in range(j * wide // B, (j + 1) * wide // B):
                 value = lax.dot_general(
                     scaled[t, :, r * B : (r + 1) * B],
@@ -233,13 +228,21 @@
     for k in range(1, chips):
         collect(k).start()
     gathered[chip] = total
+
+    def across(k, source):
+        return pltpu.make_async_remote_copy(
+            source, other.at[(chip - k + chips) % chips], sems_chip.at[4, k], sems_chip.at[5, k],
+            device_id={"cells": partner}, device_id_type=MESH,
+        )
+
+    across(0, reduced).start()
     for k in range(1, chips):
-        collect(k).wait()
-    second = pltpu.make_async_remote_copy(
-        gathered, other, sems.at[2], sems.at[3], device_id={"cells": partner}, device_id_type=MESH
-    )
-    second.start()
-    second.wait()
+        collect(k).wait_recv()
+        across(k, gathered.at[(chip - k + chips) % chips]).start()
+    for k in range(1, chips):
+        collect(k).wait_send()
+    for k in range(chips):
+        across(k, reduced).wait()
 
     eye = jnp.where(
         lax.broadcasted_iota(jnp.int32, (B, B), 0) == lax.broadcasted_iota(jnp.int32, (B, B), 1), 1.0, 0.0
@@ -296,6 +299,7 @@
             pltpu.VMEM((5, steps, cells), f32),
             pltpu.VMEM(tiles.shape, tiles.dtype),
             pltpu.VMEM((cells, 5 * cells), tiles.dtype),
+            pltpu.VMEM((cells, B), f32),
             pltpu.VMEM((steps, cells, rank), f32),
             pltpu.VMEM((2, chips, rows, wide), f32),
             pltpu.VMEM((chips, rows, wide), f32),
@@ -304,14 +308,14 @@
             pltpu.VMEM((rows, wide), f32),
             pltpu.VMEM((chips, rows, wide), f32),
             pltpu.VMEM((chips, rows, wide), f32),
-            pltpu.SemaphoreType.DMA((4,)),
-            pltpu.SemaphoreType.DMA((4, chips)),
+            pltpu.SemaphoreType.DMA((2,)),
+            pltpu.SemaphoreType.DMA((6, chips)),
             pltpu.SemaphoreType.DMA((2, 4, rank // chunk)),
             pltpu.SemaphoreType.DMA((2, 5)),
             pltpu.SemaphoreType.DMA,
         ],
         compiler_params=pltpu.CompilerParams(collective_id=0, has_side_effects=True, vmem_limit_bytes=56 << 20),
-    )(panels, filtered, tiles, neighbours, noise_var[:, None])
+    )(panels, filtered, tiles, neighbours, noise_var[None])
 
 
 def split3(v):
@@ -322,8 +326,8 @@
     return a, b, c
 
 
-def sweep_kernel(n, sections, adv_ref, inv_ref, pan_ref, pred_ref, filt_ref, noise_ref, end_ref, out_ref,
-                 later, mine, seen, passed, sem_send, sem_recv, sem_tm):
+def sweep_kernel(n, sections, adv_ref, system_ref, pan_ref, pred_ref, filt_ref, noise_ref, end_ref, out_ref,
+                 inv_ref, strip, later, mine, seen, passed, sem_send, sem_recv, sem_tm):
     me = lax.axis_index("cells")
     section = lax.axis_index("tm")
     steps = adv_ref.shape[0]
@@ -341,6 +345,9 @@
     @pl.when(has_before)
     def _():
         pl.semaphore_signal(barrier, inc=1, device_id={"tm": section - 1}, device_id_type=MESH)
+
+    for t in range(steps):
+        invert_into(system_ref.at[t], inv_ref.at[t], strip)
 
     pl.semaphore_wait(barrier, n - 1 + has_next.astype(jnp.int32) + has_before.astype(jnp.int32))
 
@@ -391,7 +398,7 @@
         handoff().wait_send()
 
 
-def sweep_back(advected, inverses, panels, predicted, filtered, noise_var, end_smoothed, n, sections):
+def sweep_back(advected, system, panels, predicted, filtered, noise_var, end_smoothed, n, sections):
     steps, cells, rank = advected.shape
     f32 = jnp.float32
     return pl.pallas_call(
@@ -400,6 +407,8 @@
         in_specs=[pl.BlockSpec(memory_space=pltpu.VMEM)] * 7,
         out_specs=pl.BlockSpec(memory_space=pltpu.VMEM),
         scratch_shapes=[
+            pltpu.VMEM((steps, rank, rank), f32),
+            pltpu.VMEM((B, rank), f32),
             pltpu.VMEM((1, cells), f32),
             pltpu.VMEM((steps, 1, rank), f32),
             pltpu.VMEM((steps, n, 1, rank), f32),
@@ -409,15 +418,14 @@
             pltpu.SemaphoreType.DMA((2,)),
         ],
         compiler_params=pltpu.CompilerParams(collective_id=1, has_side_effects=True, vmem_limit_bytes=40 << 20),
-    )(advected, inverses, panels, predicted, filtered, noise_var[None], end_smoothed[None])
+    )(advected, system, panels, predicted, filtered, noise_var[None], end_smoothed[None])
 
 
 def per_device(filtered, panels, tiles, neighbours, noise_var, end_smoothed):
     cell_devices = lax.axis_size("cells")
     system, advected, predicted = summed_system(panels, filtered, tiles, neighbours, noise_var, cell_devices)
-    inverses = jnp.stack([inverse(system[t]) for t in range(panels.shape[0])])
     return sweep_back(
-        advected, inverses, panels, predicted, filtered, noise_var, end_smoothed, cell_devices, lax.axis_size("tm")
+        advected, system, panels, predicted, filtered, noise_var, end_smoothed, cell_devices, lax.axis_size("tm")
     )
 
 

time: 103 us -> 98.6 us (0.957)
  Pallas kernels: 98.4 us -> 94.5 us
    pallas_call x1 -> x0, Pallas kernels: 23 us -> none  [inverse(): pl.pallas_call(inverse_kernel, out_shape=jax.ShapeDtypeStruct((r, r), jnp...]
    pallas_call x1, Pallas kernels: 20.6 us -> 39.7 us  [sweep_back(): pl.pallas_call(functools.partial(sweep_kernel, n, sections), out_shape=ja...]
    broadcast_in_dim x1 -> x0, local copies, waits for them, and re-layouts: 1.52 us -> none  [summed_system(): noise_var[:, None]]
    unnamed x15, local copies, waits for them, and re-layouts: 2.57 us -> 3.72 us
where the time goes in v3:
time: 98.6 us; the launch traced here: 98.3 us
  Pallas kernels  94.5 us (96%)
  local copies, waits for them, and re-layouts  3.72 us (4%)
    pallas_call x1, Pallas kernels, summed_system(): pl.pallas_call(functools.partial(gram_kernel, n), out_shape=(jax.ShapeDty...  54.8 us
    pallas_call x1, Pallas kernels, sweep_back(): pl.pallas_call(functools.partial(sweep_kernel, n, sections), out_shape=ja...  39.7 us
    unnamed x15, local copies, waits for them, and re-layouts  3.72 us

profile of v3, /device:TPU:0, one launch (start us, length us, event | category | flops | bytes accessed | tf_op | source)
XLA Modules:
  0.0 98.3 jit_solution(6832821821989615291)
XLA Ops:
  0.0 0.0 copy-start
  0.0 0.0 copy-start.3
  0.0 0.0 copy-start.5
  0.0 0.0 copy-start.4
  0.0 54.8 %shard_map.64 = (f32[1,512,512]{2,1,0:T(8,128)}, f32[1,512,512]{2,1,0:T(8,128)}, f32[1,512]{1,0:T(1,128)}) custom-call(bf16[1,512,512]{2,1,0:T(8,128)(2,1)} %pan_ref.3, f32[1,512]{1,0:T(1,128)} %filt_ref.3, bf16[2,9,256,256]{3,2,1,0:T(8,128)(2,1)} %tiles_ref.1, s32[2,9]{1,0:T(2,128)} %near_ref.1, f32[1,512]{1,0:T(1,128)} %bitcast.2), custom_call_target="tpu_custom_call" | custom-call | tf_op jit(solution)/shard_map/pallas_call | solution.py:288
  54.9 0.0 copy-done
  54.9 0.0 copy-done.3
  54.9 0.0 copy-done.5
  54.9 0.0 copy-done.4
  54.9 0.0 copy-start.1
  54.9 1.2 %copy-done.1 = f32[1,512,512]{2,1,0:T(8,128)S(1)} copy-done((f32[1,512,512]{2,1,0:T(8,128)S(1)}, f32[1,512,512]{2,1,0:T(8,128)}, u32[]{:S(2)}) %copy-start.1) | copy-done | bytes 1048600
  56.1 0.0 copy-start.2
  56.1 1.2 %copy-done.2 = f32[1,512,512]{2,1,0:T(8,128)S(1)} copy-done((f32[1,512,512]{2,1,0:T(8,128)S(1)}, f32[1,512,512]{2,1,0:T(8,128)}, u32[]{:S(2)}) %copy-start.2) | copy-done | bytes 1048600
  57.4 0.0 copy-start.6
  57.4 0.7 copy-done.6
  58.0 39.7 %shard_map.65 = f32[1,512]{1,0:T(1,128)S(1)} custom-call(f32[1,512,512]{2,1,0:T(8,128)S(1)} %copy-done.2, f32[1,512,512]{2,1,0:T(8,128)S(1)} %copy-done.1, bf16[1,512,512]{2,1,0:T(8,128)(2,1)S(1)} %copy-done, f32[1,512]{1,0:T(1,128)S(1)} %copy-done.6, f32[1,512]{1,0:T(1,128)S(1)} %copy-done.3, f32[1,512]{1,0:T(1,128)S(1)} %bitcast.3, f32[1,512]{1,0:T(1,128)S(1)} %bitcast.4), custom_call_target="tpu_custom_call" | custom-call | tf_op jit(solution)/shard_map/pallas_call | solution.py:404
  97.7 0.6 copy.8
Async XLA Ops:
  0.0 54.9 %copy-start = (bf16[1,512,512]{2,1,0:T(8,128)(2,1)S(1)}, bf16[1,512,512]{2,1,0:T(8,128)(2,1)}, u32[]{:S(2)}) copy-start(bf16[1,512,512]{2,1,0:T(8,128)(2,1)} %pan_ref.3) | copy-start | bytes 1572868
  0.0 54.9 %copy-start.3 = (f32[1,512]{1,0:T(1,128)S(1)}, f32[1,512]{1,0:T(1,128)}, u32[]{:S(2)}) copy-start(f32[1,512]{1,0:T(1,128)} %filt_ref.3) | copy-start | bytes 6148
  0.0 54.9 %copy-start.5 = (f32[512]{0:T(512)S(1)}, f32[512]{0:T(512)}, u32[]{:S(2)}) copy-start(f32[512]{0:T(512)} %param.11) | copy-start | bytes 6148
  0.0 54.9 %copy-start.4 = (f32[512]{0:T(512)S(1)}, f32[512]{0:T(512)}, u32[]{:S(2)}) copy-start(f32[512]{0:T(512)} %param.10) | copy-start | bytes 6148
  54.9 1.2 %copy-start.1 = (f32[1,512,512]{2,1,0:T(8,128)S(1)}, f32[1,512,512]{2,1,0:T(8,128)}, u32[]{:S(2)}) copy-start(f32[1,512,512]{2,1,0:T(8,128)} %get-tuple-element.9.system_ref) | copy-start | bytes 3145732
  56.1 1.2 %copy-start.2 = (f32[1,512,512]{2,1,0:T(8,128)S(1)}, f32[1,512,512]{2,1,0:T(8,128)}, u32[]{:S(2)}) copy-start(f32[1,512,512]{2,1,0:T(8,128)} %get-tuple-element.8.adv_ref) | copy-start | bytes 3145732
  57.4 0.7 copy-start.6
